TPU v7x, 256 devices: a whole 4x4x8 slice. The times are simulated.
256 devices in a mesh: row: 16 (over y, x), col: 16 (over z, core).
Axes of the slice: x: 4, y: 4, z: 8, core: 2. Of those that a mesh axis runs over, the one named last changes fastest.
Arguments:
- source: float32 [2048, 64, 128], P(('row', 'col')), may hold values from -6 to 6
- blocks: float32 [65536, 64, 64], P(('row', 'col')), may hold values from -0.15625 to 0.15625
- row_index: int32 [65536], P(('row', 'col')), may hold values from 0 to 127
- col_index: int32 [65536], P(('row', 'col')), may hold values from 0 to 127
- live_count: int32 [256], P(('row', 'col')), may hold values from 64 to 256, as said below
Outputs:
- irradiance: float32 [2048, 64, 128], P(('row', 'col'))
Inputs may be any that keep to these rules, and one draw needn't show every extreme that they name: `live_count`: slots of a device beyond its live count are padding; some device has all 256 slots live.
All inputs are finite; a program needn't handle non-finite values.
Results may differ from a plain program's by a relative error of at most 0.0003.
Values sent between devices are 32-bit elements; how exact they have to be, the bound alone decides.
A program may use at most 128 MiB of HBM per device.

v0:
```python
import jax
import jax.numpy as jnp
from jax import lax
from jax.sharding import PartitionSpec as P

ITERS = 2


def local_transfer(blocks, gathered, row_ids, col_index, group_rows):
    picked = jnp.take(gathered, col_index, axis=0)
    products = jnp.einsum("nij,njl->nil", blocks, picked, precision=lax.Precision.HIGHEST)
    summed = jax.ops.segment_sum(products, row_ids, num_segments=group_rows + 1)
    return summed[:group_rows]


def body(source, blocks, row_index, col_index, live_count):
    bricks_here = source.shape[0]
    group_rows = bricks_here * lax.axis_size("col")
    live_total = live_count[0]
    slot_ids = jnp.arange(blocks.shape[0], dtype=jnp.int32)
    row_ids = jnp.where(slot_ids < live_total, row_index, group_rows)
    field = source
    for bounce in range(ITERS):
        gathered = lax.all_gather(field, "row", axis=0, tiled=True)
        partial_value = local_transfer(blocks, gathered, row_ids, col_index, group_rows)
        whole = lax.psum(partial_value, "col")
        owned = lax.dynamic_slice_in_dim(whole, lax.axis_index("col") * bricks_here, bricks_here, 0)
        field = source + owned
    return field


def solution(mesh):
    in_specs = (
        P(("row", "col"), None, None),
        P(("row", "col"), None, None),
        P(("row", "col")),
        P(("row", "col")),
        P(("row", "col")),
    )
    out_specs = P(("row", "col"), None, None)
    return jax.shard_map(body, mesh=mesh, in_specs=in_specs, out_specs=out_specs, check_vma=False)
```

profile of v0, /device:TPU:1, one launch (start us, length us, event | category | flops | bytes accessed | tf_op | source)
XLA Modules:
  0.0 516.3 jit_solution(3725218833665404875)
XLA Ops:
  6.5 0.7 all-gather.3.cloned.1.call-update
  7.3 0.0 all-reduce.3.cloned.1.call-start
  7.3 9.2 %copy.7 = f32[256,64,64]{2,1,0:T(8,128)} copy(f32[256,64,64]{0,2,1:T(8,128)} %param.8) | data formatting | bytes 8388608 | tf_op args[1]
  17.2 52.7 %all-gather.3.cloned.1.call-done = f32[128,64,128]{2,1,0:T(8,128)} async-done(((f32[8,64,128]{2,1,0:T(8,128)}), f32[128,64,128]{2,1,0:T(8,128)}) %all-gather.3.cloned.1.call-update) | async-done | bytes 4194320 | tf_op jit(solution)/shard_map/all_gather | solution.py:24
  69.8 6.5 %gather_fusion = f32[256,64,128]{2,1,0:T(8,128)} fusion(f32[128,64,128]{2,1,0:T(8,128)} %all-gather.3.cloned.1.call-done, s32[1024]{0:T(1024)S(1)} %pad_clamp_fusion), kind=kCustom, calls=%fused_computation.clone | custom fusion | bytes 16778240 | tf_op jit(solution)/shard_map/jit(_take)/gather | solution.py:10
  76.3 14.7 %fusion.8 = f32[256,64,128]{2,1,0:T(8,128)} fusion(f32[256,64,64]{2,1,0:T(8,128)} %copy.7, f32[256,64,128]{2,1,0:T(8,128)} %gather_fusion, pred[256]{0:T(512)(128)(4,1)S(1)} %compare_and_fusion), kind=kOutput, calls=%fused_computation.12 | convolution fusion | flops 1612709888 | bytes 20971776 | tf_op jit(solution)/shard_map/nij,njl->nil/dot_general | solution.py:11
  91.0 2.5 broadcast.6.clone
  93.5 39.8 %scatter_fusion = f32[129,64,128]{2,1,0:T(8,128)} fusion(f32[129,64,128]{2,1,0:T(8,128)} %broadcast.6.clone, s32[256]{0:T(256)S(1)} %compare_select_fusion.1, f32[256,64,128]{2,1,0:T(8,128)} %fusion.8), kind=kCustom, calls=%fused_computation.2 | custom fusion | flops 2097152 | bytes 25166848 | tf_op jit(solution)/shard_map/scatter-add | solution.py:12
  133.3 4.8 slice.12
  138.1 0.0 all-reduce.3.cloned.1.call-update
  138.1 0.0 all-gather.5.cloned.1.call-start
  138.1 121.1 %all-reduce.3.cloned.1.call-done = f32[128,64,128]{2,1,0:T(8,128)} async-done(((f32[128,64,128]{2,1,0:T(8,128)}), f32[128,64,128]{2,1,0:T(8,128)}) %all-reduce.3.cloned.1.call-update) | async-done | bytes 4194320 | tf_op jit(solution)/shard_map/psum | solution.py:26
  259.3 1.7 dynamic-slice_add_fusion.1
  261.0 0.0 all-gather.5.cloned.1.call-update
  261.0 0.2 all-reduce.5.cloned.1.call-start
  261.2 57.4 %all-gather.5.cloned.1.call-done = f32[128,64,128]{2,1,0:T(8,128)} async-done(((f32[8,64,128]{2,1,0:T(8,128)}), f32[128,64,128]{2,1,0:T(8,128)}) %all-gather.5.cloned.1.call-update) | async-done | bytes 4194320 | tf_op jit(solution)/shard_map/all_gather | solution.py:24
  318.6 6.5 %gather_fusion.1 = f32[256,64,128]{2,1,0:T(8,128)} fusion(f32[128,64,128]{2,1,0:T(8,128)} %all-gather.5.cloned.1.call-done, s32[1024]{0:T(1024)S(1)} %pad_clamp_fusion), kind=kCustom, calls=%fused_computation.1.clone | custom fusion | bytes 16778240 | tf_op jit(solution)/shard_map/jit(_take)/gather | solution.py:10
  325.1 14.7 %fusion.11 = f32[256,64,128]{2,1,0:T(8,128)} fusion(f32[256,64,64]{2,1,0:T(8,128)} %copy.7, f32[256,64,128]{2,1,0:T(8,128)} %gather_fusion.1, pred[256]{0:T(512)(128)(4,1)S(1)} %compare_and_fusion), kind=kOutput, calls=%fused_computation.13 | convolution fusion | flops 1612709888 | bytes 20971776 | tf_op jit(solution)/shard_map/nij,njl->nil/dot_general | solution.py:11
  339.8 2.5 broadcast.6
  342.3 39.8 %scatter_fusion.1 = f32[129,64,128]{2,1,0:T(8,128)} fusion(f32[129,64,128]{2,1,0:T(8,128)} %broadcast.6, s32[256]{0:T(256)S(1)} %compare_select_fusion.1, f32[256,64,128]{2,1,0:T(8,128)} %fusion.11), kind=kCustom, calls=%fused_computation.3 | custom fusion | flops 2097152 | bytes 25166848 | tf_op jit(solution)/shard_map/scatter-add | solution.py:12
  382.1 4.8 slice.13
  386.8 0.0 all-reduce.5.cloned.1.call-update
  386.9 121.2 %all-reduce.5.cloned.1.call-done = f32[128,64,128]{2,1,0:T(8,128)} async-done(((f32[128,64,128]{2,1,0:T(8,128)}), f32[128,64,128]{2,1,0:T(8,128)}) %all-reduce.5.cloned.1.call-update) | async-done | bytes 4194320 | tf_op jit(solution)/shard_map/psum | solution.py:26
  508.1 1.7 dynamic-slice_add_fusion
  (11 shorter events, 0.0 us)
Async XLA Ops:
  6.5 10.6 %copy-start.1 = (s32[256]{0:T(256)S(1)}, s32[256]{0:T(256)}, u32[]{:S(2)}) copy-start(s32[256]{0:T(256)} %param.10) | copy-start | bytes 3076
  6.5 10.6 %copy-start.2 = (s32[256]{0:T(256)S(1)}, s32[256]{0:T(256)}, u32[]{:S(2)}) copy-start(s32[256]{0:T(256)} %param.9) | copy-start | bytes 3076
  6.5 63.3 %all-gather.3.cloned.1.call-start = ((), (), s32[]{:S(2)}) async-start(), calls=%async_computation | async-start | bytes 4456448 | tf_op jit(solution)/shard_map/all_gather | solution.py:24
  7.3 252.0 %all-reduce.3.cloned.1.call-start = ((), (), s32[]{:S(2)}) async-start(), calls=%async_computation.1 | async-start | bytes 8388608 | tf_op jit(solution)/shard_map/psum | solution.py:26
  133.3 126.0 %copy-start = (f32[8,64,128]{2,1,0:T(8,128)S(1)}, f32[8,64,128]{2,1,0:T(8,128)}, u32[]{:S(2)}) copy-start(f32[8,64,128]{2,1,0:T(8,128)} %param.7) | copy-start | bytes 786436
  138.1 180.5 %all-gather.5.cloned.1.call-start = ((), (), s32[]{:S(2)}) async-start(), calls=%async_computation.2 | async-start | bytes 4456448 | tf_op jit(solution)/shard_map/all_gather | solution.py:24
  261.0 247.1 %all-reduce.5.cloned.1.call-start = ((), (), s32[]{:S(2)}) async-start(), calls=%async_computation.3 | async-start | bytes 8388608 | tf_op jit(solution)/shard_map/psum | solution.py:26
Sparse Core Ops, SparseCore 0:
  9.8 60.0 all-gather.2
  138.2 121.0 all-reduce.2
  261.7 56.8 all-gather.4
  387.0 121.0 all-reduce.4
where the time goes:
time: 518 us; the launch traced here: 516 us
  waiting for transfers between devices  353 us (68%)
  other arithmetic  83 us (16%)
  local copies, waits for them, and re-layouts  36.6 us (7%)
  matrix products  29.3 us (6%)
  between operations  13.8 us (3%)
    psum x2, waiting for transfers between devices, body(): whole = lax.psum(partial_value, 'col')  242 us
    all_gather x2, waiting for transfers between devices, body(): gathered = lax.all_gather(field, 'row', axis=0, tiled=True)  110 us
    scatter-add x2, other arithmetic, local_transfer(): summed = jax.ops.segment_sum(products, row_ids, num_segments=group_rows + 1)  79.7 us
    dot_general x2, matrix products, local_transfer(): jnp.einsum('nij,njl->nil', blocks, picked, precision=lax.Precision.HIGHEST)  29.3 us
    gather x2, local copies, waits for them, and re-layouts, local_transfer(): picked = jnp.take(gathered, col_index, axis=0)  13 us
  transfers between devices with their start and end apart: 4, of which 4 were waited for; matrix products, arithmetic and copies ran while one was open for 2% of the time, Pallas kernels for 0%

commit v1 on v0

--- a/solution.py
+++ b/solution.py
@@ -23,7 +23,9 @@
     for bounce in range(ITERS):
         gathered = lax.all_gather(field, "row", axis=0, tiled=True)
         partial_value = local_transfer(blocks, gathered, row_ids, col_index, group_rows)
-        whole = lax.psum(partial_value, "col")
+        whole = partial_value
+        for hop in (1, 2, 4, 8):
+            whole = whole + lax.ppermute(whole, "col", [(dev, dev ^ hop) for dev in range(16)])
         owned = lax.dynamic_slice_in_dim(whole, lax.axis_index("col") * bricks_here, bricks_here, 0)
         field = source + owned
     return field

time: 518 us -> 1220 us (2.36)
  waiting for transfers between devices: 353 us -> 1020 us
  starting transfers between devices: 0.31 us -> 21.9 us
    ppermute x0 -> x8, waiting for transfers between devices: none -> 916 us  [body(): lax.ppermute(whole, 'col', [(dev, dev ^ hop) for dev in range(16)])]
    psum x2 -> x0, waiting for transfers between devices: 242 us -> none  [body(): whole = lax.psum(partial_value, 'col')]
    ppermute x0 -> x8, starting transfers between devices: none -> 21.8 us  [body(): lax.ppermute(whole, 'col', [(dev, dev ^ hop) for dev in range(16)])]
  transfers between devices with their start and end apart: 4 -> 10, of which waited for: 4 -> 10; matrix products, arithmetic and copies ran while one was open for 2% -> 1% of each run, Pallas kernels for 0% -> 0%
where the time goes in v1:
time: 1220 us; the launch traced here: 1210 us
  waiting for transfers between devices  1020 us (84%)
  other arithmetic  91.7 us (8%)
  local copies, waits for them, and re-layouts  32.5 us (3%)
  matrix products  29.3 us (2%)
  starting transfers between devices  21.9 us (2%)
  between operations  14.2 us (1%)
    ppermute x8, waiting for transfers between devices, body(): lax.ppermute(whole, 'col', [(dev, dev ^ hop) for dev in range(16)])  916 us
    all_gather x2, waiting for transfers between devices, body(): gathered = lax.all_gather(field, 'row', axis=0, tiled=True)  108 us
    scatter-add x2, other arithmetic, local_transfer(): summed = jax.ops.segment_sum(products, row_ids, num_segments=group_rows + 1)  79.5 us
    dot_general x2, matrix products, local_transfer(): jnp.einsum('nij,njl->nil', blocks, picked, precision=lax.Precision.HIGHEST)  29.3 us
  transfers between devices with their start and end apart: 10, of which 10 were waited for; matrix products, arithmetic and copies ran while one was open for 1% of the time, Pallas kernels for 0%

profile of v1, /device:TPU:1, one launch (start us, length us, event | category | flops | bytes accessed | tf_op | source)
XLA Modules:
  0.0 1213.7 jit_solution(4371542085471074887)
XLA Ops:
  7.3 9.2 copy.8
  17.2 52.6 %all-gather.3.cloned.1.call-done = f32[128,64,128]{2,1,0:T(8,128)} async-done(((f32[8,64,128]{2,1,0:T(8,128)}), f32[128,64,128]{2,1,0:T(8,128)}) %all-gather.3.cloned.1.call-update) | async-done | bytes 4194320 | tf_op jit(solution)/shard_map/all_gather | solution.py:24
  69.8 6.5 gather_fusion
  76.3 14.6 %fusion.8 = f32[256,64,128]{2,1,0:T(8,128)} fusion(f32[256,64,64]{2,1,0:T(8,128)} %copy.8, f32[256,64,128]{2,1,0:T(8,128)} %gather_fusion, pred[256]{0:T(512)(128)(4,1)S(1)} %compare_and_fusion), kind=kOutput, calls=%fused_computation.12 | convolution fusion | flops 1612709888 | bytes 20971776 | tf_op jit(solution)/shard_map/nij,njl->nil/dot_general | solution.py:11
  93.5 39.7 %scatter_fusion = f32[129,64,128]{2,1,0:T(8,128)} fusion(f32[129,64,128]{2,1,0:T(8,128)} %broadcast.6.clone, s32[256]{0:T(256)S(1)} %compare_select_fusion.1, f32[256,64,128]{2,1,0:T(8,128)} %fusion.8), kind=kCustom, calls=%fused_computation.2 | custom fusion | flops 2097152 | bytes 25166848 | tf_op jit(solution)/shard_map/scatter-add | solution.py:12
  133.2 2.7 slice.12
  136.4 6.8 collective-permute-done
  146.0 90.4 %collective-permute-done.1 = f32[128,64,128]{2,1,0:T(8,128)S(1)} collective-permute-done((f32[128,64,128]{2,1,0:T(8,128)S(1)}, f32[128,64,128]{2,1,0:T(8,128)S(1)}, u32[]{:S(2)}, u32[]{:S(2)}) %collective-permute-start.1) | collective-permute-done | bytes 4194336 | tf_op jit(solution)/shard_map/ppermute | solution.py:28
  237.8 3.1 collective-permute-start.2
  240.9 180.0 %collective-permute-done.2 = f32[128,64,128]{2,1,0:T(8,128)S(1)} collective-permute-done((f32[128,64,128]{2,1,0:T(8,128)S(1)}, f32[128,64,128]{2,1,0:T(8,128)S(1)}, u32[]{:S(2)}, u32[]{:S(2)}) %collective-permute-start.2) | collective-permute-done | bytes 4194336 | tf_op jit(solution)/shard_map/ppermute | solution.py:28
  420.9 2.9 add.46
  423.8 5.9 collective-permute-start.3
  429.7 180.9 %collective-permute-done.3 = f32[128,64,128]{2,1,0:T(8,128)} collective-permute-done((f32[128,64,128]{2,1,0:T(8,128)}, f32[128,64,128]{2,1,0:T(8,128)}, u32[]{:S(2)}, u32[]{:S(2)}) %collective-permute-start.3) | collective-permute-done | bytes 4194336 | tf_op jit(solution)/shard_map/ppermute | solution.py:28
  612.4 55.2 %all-gather.5.cloned.1.call-done = f32[128,64,128]{2,1,0:T(8,128)} async-done(((f32[8,64,128]{2,1,0:T(8,128)}), f32[128,64,128]{2,1,0:T(8,128)}) %all-gather.5.cloned.1.call-update) | async-done | bytes 4194320 | tf_op jit(solution)/shard_map/all_gather | solution.py:24
  667.6 6.5 gather_fusion.1
  674.1 14.6 %fusion.11 = f32[256,64,128]{2,1,0:T(8,128)} fusion(f32[256,64,64]{2,1,0:T(8,128)} %copy.8, f32[256,64,128]{2,1,0:T(8,128)} %gather_fusion.1, pred[256]{0:T(512)(128)(4,1)S(1)} %compare_and_fusion), kind=kOutput, calls=%fused_computation.13 | convolution fusion | flops 1612709888 | bytes 20971776 | tf_op jit(solution)/shard_map/nij,njl->nil/dot_general | solution.py:11
  691.3 39.7 %scatter_fusion.1 = f32[129,64,128]{2,1,0:T(8,128)} fusion(f32[129,64,128]{2,1,0:T(8,128)} %broadcast.6, s32[256]{0:T(256)S(1)} %compare_select_fusion.1, f32[256,64,128]{2,1,0:T(8,128)} %fusion.11), kind=kCustom, calls=%fused_computation.3 | custom fusion | flops 2097152 | bytes 25166848 | tf_op jit(solution)/shard_map/scatter-add | solution.py:12
  731.0 2.7 slice.13
  734.2 6.8 collective-permute-done.4
  743.7 90.4 %collective-permute-done.5 = f32[128,64,128]{2,1,0:T(8,128)S(1)} collective-permute-done((f32[128,64,128]{2,1,0:T(8,128)S(1)}, f32[128,64,128]{2,1,0:T(8,128)S(1)}, u32[]{:S(2)}, u32[]{:S(2)}) %collective-permute-start.5) | collective-permute-done | bytes 4194336 | tf_op jit(solution)/shard_map/ppermute | solution.py:28
  835.5 3.0 collective-permute-start.6
  838.6 180.0 %collective-permute-done.6 = f32[128,64,128]{2,1,0:T(8,128)S(1)} collective-permute-done((f32[128,64,128]{2,1,0:T(8,128)S(1)}, f32[128,64,128]{2,1,0:T(8,128)S(1)}, u32[]{:S(2)}, u32[]{:S(2)}) %collective-permute-start.6) | collective-permute-done | bytes 4194336 | tf_op jit(solution)/shard_map/ppermute | solution.py:28
  1019.9 5.8 collective-permute-start.7
  1025.8 180.4 %collective-permute-done.7 = f32[128,64,128]{2,1,0:T(8,128)S(1)} collective-permute-done((f32[128,64,128]{2,1,0:T(8,128)S(1)}, f32[128,64,128]{2,1,0:T(8,128)S(1)}, u32[]{:S(2)}, u32[]{:S(2)}) %collective-permute-start.7) | collective-permute-done | bytes 4194336 | tf_op jit(solution)/shard_map/ppermute | solution.py:28
  (31 shorter events, 19.0 us)
Async XLA Ops:
  6.5 63.3 %all-gather.3.cloned.1.call-start = ((), (), s32[]{:S(2)}) async-start(), calls=%async_computation | async-start | bytes 4456448 | tf_op jit(solution)/shard_map/all_gather | solution.py:24
  7.3 9.9 copy-start.3
  7.3 9.9 copy-start.4
  7.3 660.3 %all-gather.5.cloned.1.call-start = ((), (), s32[]{:S(2)}) async-start(), calls=%async_computation.1 | async-start | bytes 4456448 | tf_op jit(solution)/shard_map/all_gather | solution.py:24
  133.2 10.0 copy-start.1
  135.9 7.3 collective-permute-start
  144.6 91.8 %collective-permute-start.1 = (f32[128,64,128]{2,1,0:T(8,128)S(1)}, f32[128,64,128]{2,1,0:T(8,128)S(1)}, u32[]{:S(2)}, u32[]{:S(2)}) collective-permute-start(f32[128,64,128]{2,1,0:T(8,128)S(1)} %slice_add_fusion.1), channel_id=1, source_target_pairs={{0,2},{1,3},{2,0},{3,1},{4,6},{5,7},{6,4},{7,5},{8,10},{9,11},{10,... | collective-permute-start | bytes 12582920 | tf_op jit(solution)/shard_map/ppermute | solution.py:28
  237.8 372.9 %copy-start.2 = (f32[8,64,128]{2,1,0:T(8,128)S(1)}, f32[8,64,128]{2,1,0:T(8,128)}, u32[]{:S(2)}) copy-start(f32[8,64,128]{2,1,0:T(8,128)} %param.7) | copy-start | bytes 786436
  237.8 183.1 %collective-permute-start.2 = (f32[128,64,128]{2,1,0:T(8,128)S(1)}, f32[128,64,128]{2,1,0:T(8,128)S(1)}, u32[]{:S(2)}, u32[]{:S(2)}) collective-permute-start(f32[128,64,128]{2,1,0:T(8,128)S(1)} %add.45), channel_id=1, source_target_pairs={{0,4},{1,5},{2,6},{3,7},{4,0},{5,1},{6,2},{7,3},{8,12},{9,13},{10,... | collective-permute-start | bytes 12582920 | tf_op jit(solution)/shard_map/ppermute | solution.py:28
  423.8 186.8 %collective-permute-start.3 = (f32[128,64,128]{2,1,0:T(8,128)}, f32[128,64,128]{2,1,0:T(8,128)}, u32[]{:S(2)}, u32[]{:S(2)}) collective-permute-start(f32[128,64,128]{2,1,0:T(8,128)} %add.46), channel_id=1, source_target_pairs={{0,8},{1,9},{2,10},{3,11},{4,12},{5,13},{6,14},{7,15},{8,0},{9,1},... | collective-permute-start | bytes 12582920 | tf_op jit(solution)/shard_map/ppermute | solution.py:28
  731.0 9.9 copy-start
  733.7 7.3 collective-permute-start.4
  742.3 91.8 %collective-permute-start.5 = (f32[128,64,128]{2,1,0:T(8,128)S(1)}, f32[128,64,128]{2,1,0:T(8,128)S(1)}, u32[]{:S(2)}, u32[]{:S(2)}) collective-permute-start(f32[128,64,128]{2,1,0:T(8,128)S(1)} %slice_add_fusion), channel_id=1, source_target_pairs={{0,2},{1,3},{2,0},{3,1},{4,6},{5,7},{6,4},{7,5},{8,10},{9,11},{10,... | collective-permute-start | bytes 12582920 | tf_op jit(solution)/shard_map/ppermute | solution.py:28
  835.5 183.0 %collective-permute-start.6 = (f32[128,64,128]{2,1,0:T(8,128)S(1)}, f32[128,64,128]{2,1,0:T(8,128)S(1)}, u32[]{:S(2)}, u32[]{:S(2)}) collective-permute-start(f32[128,64,128]{2,1,0:T(8,128)S(1)} %add.51), channel_id=1, source_target_pairs={{0,4},{1,5},{2,6},{3,7},{4,0},{5,1},{6,2},{7,3},{8,12},{9,13},{10,... | collective-permute-start | bytes 12582920 | tf_op jit(solution)/shard_map/ppermute | solution.py:28
  1019.9 186.2 %collective-permute-start.7 = (f32[128,64,128]{2,1,0:T(8,128)S(1)}, f32[128,64,128]{2,1,0:T(8,128)S(1)}, u32[]{:S(2)}, u32[]{:S(2)}) collective-permute-start(f32[128,64,128]{2,1,0:T(8,128)S(1)} %add.52), channel_id=1, source_target_pairs={{0,8},{1,9},{2,10},{3,11},{4,12},{5,13},{6,14},{7,15},{8,0},{9,1},... | collective-permute-start | bytes 12582920 | tf_op jit(solution)/shard_map/ppermute | solution.py:28
Sparse Core Ops, SparseCore 0:
  9.8 60.0 all-gather.2
  612.5 55.0 all-gather.4
